TPU v7x, 32 devices: a whole 2x2x4 slice. The times are simulated.
32 devices in a mesh: copies: 2 (over y), blk: 4 (over x, core), virt: 4 (over z).
Axes of the slice: x: 2, y: 2, z: 4, core: 2. Of those that a mesh axis runs over, the one named last changes fastest.
Arguments:
- three_index: bfloat16 [32, 512, 2048], P(('copies', 'blk'), 'virt'), parts along dimension 0, may hold values from -0.59765625 to 0.59765625
- occ_energy: float32 [32], P(('copies', 'blk')), parts along dimension 0, may hold values from -2 to -0.5
- virt_energy: float32 [1024], P('copies'), parts along dimension 0, may hold values from 0.3 to 3
Outputs:
- gradient: bfloat16 [32, 512, 2048], P(('copies', 'blk'), 'virt'), parts along dimension 0
There are 2 independent parts, one for each index of `copies`. A program takes and returns all parts, laid end to end along the dimension named above; each array names one. Nothing has to cross between parts.
All inputs are finite; a program needn't handle non-finite values.
Results may differ from a plain program's by a relative error of at most 0.0055.
Values may be sent and summed in bfloat16 or wider, within the bound.
A program may use at most 64 MiB of HBM per device.

v0:
```python
import functools

import jax
import jax.numpy as jnp
from jax import lax
from jax.experimental import pallas as pl
from jax.experimental.pallas import tpu as pltpu
from jax.sharding import PartitionSpec as P

MESH = pl.DeviceIdType.MESH
SEND_COLUMNS = 256
SUM_COLUMNS = 512


def shifted(shard, axis, by):
    devices = lax.axis_size(axis)
    return lax.ppermute(shard, axis, [(i, (i + by) % devices) for i in range(devices)])


def contract(left, right):
    return lax.dot_general(
        left, right, (((1,), (1,)), ((), ())), preferred_element_type=jnp.float32
    )


def plain_local(three_index, occ_energy, virt_energy):
    occ, rows, aux = three_index.shape
    virt = virt_energy.shape[0]
    energy_rows = lax.dynamic_slice_in_dim(virt_energy, lax.axis_index("virt") * rows, rows, 0)
    part_rows = shifted(three_index, "blk", 1)
    own_full = lax.all_gather(three_index, "virt", axis=1, tiled=True)
    part_full = shifted(own_full, "blk", 1)
    energy_part = shifted(occ_energy, "blk", 1)

    def pairs(left, right):
        both = contract(left.reshape(occ * rows, aux), right.reshape(occ * virt, aux))
        return both.reshape(occ, rows, occ, virt)

    def denominator(left, right):
        return (
            left[:, None, None, None]
            + right[None, None, :, None]
            - energy_rows[None, :, None, None]
            - virt_energy[None, None, None, :]
        )

    def spread(tbar, full):
        return jnp.dot(
            tbar.astype(jnp.bfloat16).reshape(occ * rows, occ * virt),
            full.reshape(occ * virt, aux),
            preferred_element_type=jnp.float32,
        ).reshape(occ, rows, aux)

    diag = pairs(three_index, own_full)
    first = pairs(three_index, part_full)
    second = pairs(part_rows, own_full)
    own = spread(
        (2.0 * diag - diag.transpose(2, 1, 0, 3)) / denominator(occ_energy, occ_energy), own_full
    )
    own += spread(
        (2.0 * first - second.transpose(2, 1, 0, 3)) / denominator(occ_energy, energy_part),
        part_full,
    )
    partner = spread(
        (2.0 * second - first.transpose(2, 1, 0, 3)) / denominator(energy_part, occ_energy),
        own_full,
    ).astype(jnp.bfloat16)
    partner = shifted(partner, "blk", -1)
    return (own + partner.astype(jnp.float32)).astype(jnp.bfloat16)


def kernel(
    blocks,
    a_ref,
    e_ref,
    row_ref,
    o_ref,
    own_full,
    part_full,
    e_part,
    column_ref,
    acc,
    pacc,
    racc,
    psend,
    precv,
    hsend,
    hrecv,
    rsend,
    rrecv,
    k_ref,
    x_ref,
    td_ref,
    tu_ref,
    t_ref,
    staged,
    send_in,
    send_out,
    send_next,
    send_part,
    recv_own,
    recv_part,
    back_sems,
    help_sems,
    result_sems,
    e_sems,
    out_sems,
    local_sem,
):
    occ, rows, aux = a_ref.shape
    size = occ * rows
    cuts = 2 * occ
    ahead = 3
    chunks = range(aux // SEND_COLUMNS)
    v = lax.axis_index("virt")
    g = lax.axis_index("blk")
    after = lax.rem(g + 1, blocks)
    before = lax.rem(g + blocks - 1, blocks)
    step = jnp.where(v < 2, 1, -1)
    middle = (v == 1) | (v == 2)
    even = lax.rem(g, 2) == 0
    end = (v == 0) | (v == 3)
    inner = v + step
    outer = lax.rem(v - step + 4, 4)
    far = lax.rem(v + 2 * step + 4, 4)
    near = jnp.where(middle, outer, inner)
    last = jnp.where(middle, inner, far)

    def remote(src, dst, send, recv, **where):
        return pltpu.make_async_remote_copy(
            src_ref=src, dst_ref=dst, send_sem=send, recv_sem=recv,
            device_id=where, device_id_type=MESH,
        )

    def piece(ref, *lead):
        *lead, c = lead
        cols = slice((c % 2) * (aux // 2), (c % 2 + 1) * (aux // 2))
        return ref.at[(*lead, c // 2, slice(None), cols)]

    def to_inner(s, c):
        return remote(
            piece(own_full, s, c), piece(own_full, s, c), send_in.at[s, c], recv_own.at[s, c], virt=inner
        )

    def to_outer(s, c):
        return remote(
            piece(own_full, s, c), piece(own_full, s, c), send_out.at[s, c], recv_own.at[s, c], virt=outer
        )

    def to_next(s, c):
        return remote(
            piece(own_full, s, c), piece(part_full, s, c), send_next.at[s, c], recv_part.at[s, c],
            blk=after,
        )

    def part_to_inner(c):
        return remote(
            piece(part_full, v, c), piece(part_full, v, c), send_part.at[c], recv_part.at[v, c],
            virt=inner,
        )

    def back(k):
        return remote(
            psend.at[k], precv.at[k], back_sems.at[0, k], back_sems.at[1, k], blk=before
        )

    def help_back(k):
        return remote(
            hsend.at[k], hrecv.at[k], help_sems.at[0, k], help_sems.at[1, k], blk=before
        )

    def result(k):
        return remote(
            rsend.at[k], rrecv.at[k], result_sems.at[0, k], result_sems.at[1, k], virt=outer
        )

    def own_copy(make, send, c):
        return remote(
            piece(a_ref, c), piece(make, v, c), send.at[v, c],
            (recv_part if make is part_full else recv_own).at[v, c],
            **({"blk": after} if make is part_full else {"virt": inner if send is send_in else outer}),
        )

    def write(k):
        cols = slice(k * SEND_COLUMNS, (k + 1) * SEND_COLUMNS)
        return pltpu.make_async_copy(staged.at[k], o_ref.at[:, :, cols], out_sems.at[k])

    energy_copy = remote(e_ref, e_part, e_sems.at[0], e_sems.at[1], blk=after)
    keep = pltpu.make_async_copy(a_ref, own_full.at[v], local_sem)

    barrier = pltpu.get_barrier_semaphore()
    pl.semaphore_signal(barrier, inc=1, device_id={"blk": after}, device_id_type=MESH)
    pl.semaphore_signal(barrier, inc=1, device_id={"blk": before}, device_id_type=MESH)
    pl.semaphore_signal(barrier, inc=1, device_id={"virt": inner}, device_id_type=MESH)

    @pl.when(middle)
    def _():
        pl.semaphore_signal(barrier, inc=1, device_id={"virt": outer}, device_id_type=MESH)

    pl.semaphore_wait(barrier, 3 + middle.astype(jnp.int32))

    for c in range(ahead):
        own_copy(own_full, send_in, c).start()
    for c in range(ahead, cuts):
        @pl.when(end)
        def _():
            own_copy(own_full, send_in, c).start()
    for c in range(cuts):
        @pl.when(middle)
        def _():
            own_copy(own_full, send_out, c).start()
    energy_copy.start()
    for c in range(cuts):
        own_copy(part_full, send_next, c).start()
    keep.start()
    for s in range(4):
        column_ref[s] = jnp.transpose(jnp.broadcast_to(row_ref[s], (rows, rows)))[:, 0:1]
    keep.wait()

    def inverse(left, i, right, j, r, s):
        return 1.0 / (
            (left[0:1, i : i + 1] + right[0:1, j : j + 1]) - column_ref[r] - row_ref[s]
        )

    def at(i):
        return slice(i * rows, (i + 1) * rows)

    def product(left, source, s, cols, width):
        return jnp.dot(
            left[...], source[s, :, :, cols].reshape(size, width),
            preferred_element_type=jnp.float32,
        )

    def add_columns(total, left, source, s, first):
        @pl.loop(0, aux // SUM_COLUMNS)
        def _(k):
            cols = pl.ds(pl.multiple_of(k * SUM_COLUMNS, SUM_COLUMNS), SUM_COLUMNS)
            value = product(left, source, s, cols, SUM_COLUMNS)
            if first:
                total[:, cols] = value
            else:
                total[:, cols] += value

    def shard(source, s):
        return source[s].reshape(size, aux)

    def part_arrives(s):
        for c in range(cuts):
            to_next(s, c).wait_recv()

    def pair_ratio(r, s, ratio_ref):
        k_ref[...] = contract(shard(own_full, r), shard(own_full, s))
        for i in range(occ):
            for j in range(occ):
                ratio_ref[at(i), at(j)] = (
                    (2.0 * k_ref[at(i), at(j)] - k_ref[at(j), at(i)])
                    * inverse(e_ref, i, e_ref, j, r, s)
                ).astype(jnp.bfloat16)

    def diagonal(r, s, total, first):
        pair_ratio(r, s, tu_ref)
        add_columns(total, tu_ref, own_full, s, first)

    def cross(r, s, wait):
        k_ref[...] = contract(shard(part_full, r), shard(own_full, s))
        if wait:
            part_arrives(s)
        x_ref[...] = contract(shard(own_full, r), shard(part_full, s))
        amplitudes(r, s)

    def amplitudes(r, s):
        for i in range(occ):
            for j in range(occ):
                scale = inverse(e_ref, i, e_part, j, r, s)
                x = x_ref[at(i), at(j)]
                y = k_ref[at(j), at(i)]
                t_ref[at(i), at(j)] = ((2.0 * x - y) * scale).astype(jnp.bfloat16)
                tu_ref[at(j), at(i)] = ((2.0 * y - x) * scale).astype(jnp.bfloat16)

    def spread(s, first):
        add_columns(pacc, tu_ref, own_full, s, first)
        add_columns(acc, t_ref, part_full, s, False)

    def from_outer(c):
        to_outer(outer, c).wait_recv()
        to_inner(outer, c).start()

        @pl.when(even)
        def _():
            to_next(outer, c).start()

    def from_partner(c):
        to_inner(inner, c).wait_recv()
        to_outer(inner, c).start()
        to_next(inner, c).start()

    def from_far(c):
        to_inner(far, c).wait_recv()
        to_next(far, c).start()

    def from_inner(s, c):
        to_inner(s, c).wait_recv()
        to_next(s, c).start()

    diagonal(v, v, acc, True)
    energy_copy.wait_recv()

    for c in range(occ):
        @pl.when(middle)
        def _():
            from_outer(c)
            if c < ahead:
                from_partner(c)

        @pl.when(end)
        def _():
            from_inner(inner, c)

    part_arrives(v)

    @pl.when(end & even)
    def _():
        for c in range(cuts):
            part_to_inner(c).start()

    cross(v, v, False)
    spread(v, True)

    for c in range(occ, cuts):
        @pl.when(middle)
        def _():
            from_outer(c)

        @pl.when(end)
        def _():
            from_inner(inner, c)

    @pl.when(middle)
    def _():
        for c in range(ahead, cuts):
            own_copy(own_full, send_in, c).start()
        for c in range(occ):
            from_far(c)

    diagonal(v, near, acc, False)

    @pl.when(middle)
    def _():
        for c in range(occ, cuts - 1):
            from_far(c)

    @pl.when(end)
    def _():
        cross(v, near, True)
        spread(near, False)

    @pl.when(middle)
    def _():
        from_far(cuts - 1)
        pair_ratio(outer, far, td_ref)
        from_partner(ahead)
        part_arrives(outer)
        cross(outer, far, True)
        from_partner(ahead + 1)
        for k in chunks:
            cols = slice(k * SEND_COLUMNS, (k + 1) * SEND_COLUMNS)
            hsend[k] = product(tu_ref, own_full, far, cols, SEND_COLUMNS).astype(jnp.bfloat16)
            help_back(k).start()
        from_partner(ahead + 2)

        @pl.loop(0, aux // SUM_COLUMNS)
        def _(k):
            cols = pl.ds(pl.multiple_of(k * SUM_COLUMNS, SUM_COLUMNS), SUM_COLUMNS)
            racc[:, cols] = product(td_ref, own_full, far, cols, SUM_COLUMNS) + product(
                t_ref, part_full, far, cols, SUM_COLUMNS
            )

        for c in range(ahead + 3, cuts - 1):
            from_partner(c)
        diagonal(v, far, acc, False)
        from_partner(cuts - 1)
        for k in chunks:
            cols = slice(k * SEND_COLUMNS, (k + 1) * SEND_COLUMNS)
            help_back(k).wait_recv()
            rsend[k] = (racc[:, cols] + hrecv[k].astype(jnp.float32)).astype(jnp.bfloat16)
            result(k).start()
        cross(v, outer, False)
        spread(outer, False)
        cross(v, far, False)
        spread(far, False)

    @pl.when(end)
    def _():
        for c in range(cuts):
            from_inner(far, c)

    diagonal(v, last, acc, False)
    cross(v, last, True)
    for k in chunks:
        cols = slice(k * SEND_COLUMNS, (k + 1) * SEND_COLUMNS)
        psend[k] = (
            pacc[:, cols] + product(tu_ref, own_full, last, cols, SEND_COLUMNS)
        ).astype(jnp.bfloat16)
        back(k).start()
    add_columns(acc, t_ref, part_full, last, False)
    for k in chunks:
        cols = slice(k * SEND_COLUMNS, (k + 1) * SEND_COLUMNS)

        @pl.when(end)
        def _():
            result(k).wait_recv()
            acc[:, cols] += rrecv[k].astype(jnp.float32)

        back(k).wait_recv()
        staged[k] = (
            (acc[:, cols] + precv[k].astype(jnp.float32))
            .astype(jnp.bfloat16)
            .reshape(occ, rows, SEND_COLUMNS)
        )
        write(k).start()

    energy_copy.wait_send()
    for k in chunks:
        back(k).wait_send()
        write(k).wait()
    for c in range(cuts):
        for s in (v, inner, far):
            to_next(s, c).wait_send()
        to_inner(v, c).wait_send()

        @pl.when(middle)
        def _():
            to_inner(outer, c).wait_send()
            to_outer(v, c).wait_send()
            to_outer(inner, c).wait_send()

        @pl.when(middle & even)
        def _():
            to_next(outer, c).wait_send()

        @pl.when(end & even)
        def _():
            part_to_inner(c).wait_send()

    @pl.when(middle)
    def _():
        for k in chunks:
            help_back(k).wait_send()
            result(k).wait_send()


def fused_local(three_index, occ_energy, virt_energy):
    occ, rows, aux = three_index.shape
    members, blocks = lax.axis_size("virt"), lax.axis_size("blk")
    size, parts = occ * rows, aux // SEND_COLUMNS
    vmem = pl.BlockSpec(memory_space=pltpu.VMEM)
    dma = pltpu.SemaphoreType.DMA
    full = pltpu.VMEM((members, occ, rows, aux), jnp.bfloat16)
    total = pltpu.VMEM((size, aux), jnp.float32)
    pieces = pltpu.VMEM((parts, size, SEND_COLUMNS), jnp.bfloat16)
    return pl.pallas_call(
        functools.partial(kernel, blocks),
        out_shape=jax.ShapeDtypeStruct((occ, rows, aux), jnp.bfloat16),
        in_specs=[pl.BlockSpec(memory_space=pl.ANY), vmem, vmem],
        out_specs=pl.BlockSpec(memory_space=pl.ANY),
        scratch_shapes=[
            full,
            full,
            pltpu.VMEM((1, occ), jnp.float32),
            pltpu.VMEM((members, rows, 1), jnp.float32),
            *[total] * 3,
            *[pieces] * 6,
            *[pltpu.VMEM((size, size), jnp.float32)] * 2,
            *[pltpu.VMEM((size, size), jnp.bfloat16)] * 3,
            pltpu.VMEM((parts, occ, rows, SEND_COLUMNS), jnp.bfloat16),
            *[dma((members, 2 * occ))] * 3,
            dma((2 * occ,)),
            *[dma((members, 2 * occ))] * 2,
            *[dma((2, parts))] * 3,
            dma((2,)),
            dma((parts,)),
            dma,
        ],
        compiler_params=pltpu.CompilerParams(
            collective_id=0, has_side_effects=True, vmem_limit_bytes=63 * 2**20
        ),
    )(three_index, occ_energy.reshape(1, occ), virt_energy.reshape(members, 1, rows))


def local(three_index, occ_energy, virt_energy):
    occ, rows, aux = three_index.shape
    tiles = rows % 128 == 0 and aux % SUM_COLUMNS == 0 and occ >= 4
    if tiles and lax.axis_size("virt") == 4 and lax.axis_size("blk") % 2 == 0:
        return fused_local(three_index, occ_energy, virt_energy)
    return plain_local(three_index, occ_energy, virt_energy)


def solution(mesh):
    placed = (P(("copies", "blk"), "virt", None), P(("copies", "blk")), P("copies"))
    return jax.shard_map(
        local,
        mesh=mesh,
        in_specs=placed,
        out_specs=P(("copies", "blk"), "virt", None),
        check_vma=False,
    )
```

profile of v0, /device:TPU:0, one launch (start us, length us, event | category | flops | bytes accessed | tf_op | source)
XLA Modules:
  0.0 154.9 jit_solution(4824815405934141500)
XLA Ops:
  0.0 151.7 %shard_map.37 = bf16[4,128,2048]{2,1,0:T(8,128)(2,1)} custom-call(bf16[4,128,2048]{2,1,0:T(8,128)(2,1)} %a_ref.1, f32[1,4]{1,0:T(1,128)} %bitcast.3, f32[4,1,128]{2,1,0:T(1,128)} %bitcast.2), custom_call_target="tpu_custom_call" | custom-call | tf_op jit(solution)/shard_map/pallas_call | solution.py:461
  151.7 3.2 %copy.5 = bf16[4,128,2048]{2,1,0:T(8,128)(2,1)} copy(bf16[4,128,2048]{2,1,0:T(8,128)(2,1)} %shard_map.37) | data formatting | bytes 4194304
where the time goes:
time: 155 us
  Pallas kernels  152 us (98%)
  local copies, waits for them, and re-layouts  3.16 us (2%)
    pallas_call x1, Pallas kernels, fused_local(): pl.pallas_call(functools.partial(kernel, blocks), out_shape=jax.ShapeDtyp...  152 us
    unnamed x1, local copies, waits for them, and re-layouts  3.16 us

commit v1 on v0

v1 whole, which is shorter than its diff:
```python
import functools

import jax
import jax.numpy as jnp
from jax import lax
from jax.experimental import pallas as pl
from jax.experimental.pallas import tpu as pltpu
from jax.sharding import PartitionSpec as P

MESH = pl.DeviceIdType.MESH
SEND_COLUMNS = 256
SUM_COLUMNS = 1024


def shifted(shard, axis, by):
    devices = lax.axis_size(axis)
    return lax.ppermute(shard, axis, [(i, (i + by) % devices) for i in range(devices)])


def contract(left, right):
    return lax.dot_general(
        left, right, (((1,), (1,)), ((), ())), preferred_element_type=jnp.float32
    )


def plain_local(three_index, occ_energy, virt_energy):
    occ, rows, aux = three_index.shape
    virt = virt_energy.shape[0]
    energy_rows = lax.dynamic_slice_in_dim(virt_energy, lax.axis_index("virt") * rows, rows, 0)
    part_rows = shifted(three_index, "blk", 1)
    own_full = lax.all_gather(three_index, "virt", axis=1, tiled=True)
    part_full = shifted(own_full, "blk", 1)
    energy_part = shifted(occ_energy, "blk", 1)

    def pairs(left, right):
        both = contract(left.reshape(occ * rows, aux), right.reshape(occ * virt, aux))
        return both.reshape(occ, rows, occ, virt)

    def denominator(left, right):
        return (
            left[:, None, None, None]
            + right[None, None, :, None]
            - energy_rows[None, :, None, None]
            - virt_energy[None, None, None, :]
        )

    def spread(tbar, full):
        return jnp.dot(
            tbar.astype(jnp.bfloat16).reshape(occ * rows, occ * virt),
            full.reshape(occ * virt, aux),
            preferred_element_type=jnp.float32,
        ).reshape(occ, rows, aux)

    diag = pairs(three_index, own_full)
    first = pairs(three_index, part_full)
    second = pairs(part_rows, own_full)
    own = spread(
        (2.0 * diag - diag.transpose(2, 1, 0, 3)) / denominator(occ_energy, occ_energy), own_full
    )
    own += spread(
        (2.0 * first - second.transpose(2, 1, 0, 3)) / denominator(occ_energy, energy_part),
        part_full,
    )
    partner = spread(
        (2.0 * second - first.transpose(2, 1, 0, 3)) / denominator(energy_part, occ_energy),
        own_full,
    ).astype(jnp.bfloat16)
    partner = shifted(partner, "blk", -1)
    return (own + partner.astype(jnp.float32)).astype(jnp.bfloat16)


def kernel(
    blocks,
    a_ref,
    e_ref,
    row_ref,
    o_ref,
    own_full,
    part_full,
    near,
    e_part,
    column_ref,
    tot,
    ptot,
    psend,
    precv,
    hsend,
    hrecv,
    rsend,
    rrecv,
    rel,
    k_ref,
    x_ref,
    td_ref,
    tu_ref,
    t_ref,
    staged,
    send_in,
    send_out,
    send_next,
    send_part,
    recv_own,
    recv_part,
    side_sems,
    pass_sems,
    back_sems,
    help_sems,
    result_sems,
    rel_sems,
    e_sems,
    out_sems,
    local_sem,
):
    occ, rows, aux = a_ref.shape
    size = occ * rows
    half = aux // 2
    cuts = 2 * occ
    parts = aux // SEND_COLUMNS
    chunks = range(parts)
    v = lax.axis_index("virt")
    g = lax.axis_index("blk")
    copy = lax.axis_index("copies")
    other = 1 - copy
    after = lax.rem(g + 1, blocks)
    before = lax.rem(g + blocks - 1, blocks)
    middle = (v == 1) | (v == 2)
    end = (v == 0) | (v == 3)
    even = lax.rem(g, 2) == 0
    full = copy == 0
    lean = copy == 1
    adj = v + 1 - 2 * lax.rem(v, 2)
    mid = jnp.where(v < 2, 2, 1)
    tip = jnp.where(v < 2, 3, 0)
    inner = jnp.where(middle, mid, adj)
    helper = middle & lean
    served = end & lean
    gathers = jnp.logical_not(served)

    def remote(src, dst, send, recv, **where):
        return pltpu.make_async_remote_copy(
            src_ref=src, dst_ref=dst, send_sem=send, recv_sem=recv,
            device_id=where, device_id_type=MESH,
        )

    def piece(ref, *lead):
        *lead, c = lead
        if isinstance(c, int):
            i, cols = c // 2, slice((c % 2) * half, (c % 2 + 1) * half)
        else:
            i, cols = c // 2, pl.ds(pl.multiple_of(lax.rem(c, 2) * half, half), half)
        return ref.at[(*lead, i, slice(None), cols)]

    def to_inner(s, c):
        return remote(
            piece(own_full, s, c), piece(own_full, s, c), send_in.at[s, c], recv_own.at[s, c], virt=inner
        )

    def to_outer(s, c):
        return remote(
            piece(own_full, s, c), piece(own_full, s, c), send_out.at[s, c], recv_own.at[s, c], virt=adj
        )

    def to_next(s, c):
        return remote(
            piece(own_full, s, c), piece(part_full, s, c), send_next.at[s, c], recv_part.at[s, c],
            blk=after,
        )

    def part_to_inner(c):
        return remote(
            piece(part_full, v, c), piece(part_full, v, c), send_part.at[c], recv_part.at[v, c],
            virt=adj,
        )

    def own_inner(c):
        return remote(
            piece(a_ref, c), piece(own_full, v, c), send_in.at[v, c], recv_own.at[v, c], virt=inner
        )

    def own_next(c):
        return remote(
            piece(a_ref, c), piece(part_full, v, c), send_next.at[v, c], recv_part.at[v, c], blk=after
        )

    def own_side(c):
        return remote(
            piece(a_ref, c), piece(near, c), side_sems.at[0, c], side_sems.at[1, c], copies=other
        )

    def pass_side(c):
        return remote(
            piece(near, c), piece(own_full, v, c), pass_sems.at[c], recv_own.at[v, c],
            copies=other, virt=adj,
        )

    def back(k):
        return remote(
            psend.at[k], precv.at[k], back_sems.at[0, k], back_sems.at[1, k], blk=before
        )

    def help_back(k):
        return remote(
            hsend.at[k], hrecv.at[k], help_sems.at[0, k], help_sems.at[1, k], blk=before
        )

    def by_side(k):
        return k % 2 == 1

    def result(k):
        if by_side(k):
            return remote(
                rsend.at[k], rel.at[k // 2], result_sems.at[0, k], rel_sems.at[0, k // 2], copies=other
            )
        return remote(
            rsend.at[k], rrecv.at[k], result_sems.at[0, k], result_sems.at[1, k], virt=adj
        )

    def pass_result(k):
        return remote(
            rel.at[k // 2], rrecv.at[k], rel_sems.at[1, k // 2], result_sems.at[1, k],
            copies=other, virt=adj,
        )

    def write(k):
        cols = slice(k * SEND_COLUMNS, (k + 1) * SEND_COLUMNS)
        return pltpu.make_async_copy(staged.at[k], o_ref.at[:, :, cols], out_sems.at[k])

    energy_copy = remote(e_ref, e_part, e_sems.at[0], e_sems.at[1], blk=after)
    keep = pltpu.make_async_copy(a_ref, own_full.at[v], local_sem)

    barrier = pltpu.get_barrier_semaphore()
    pl.semaphore_signal(barrier, inc=1, device_id={"blk": after}, device_id_type=MESH)
    pl.semaphore_signal(barrier, inc=1, device_id={"blk": before}, device_id_type=MESH)
    pl.semaphore_signal(barrier, inc=1, device_id={"virt": adj}, device_id_type=MESH)
    pl.semaphore_signal(barrier, inc=1, device_id={"copies": other, "virt": adj}, device_id_type=MESH)

    @pl.when(middle)
    def _():
        pl.semaphore_signal(barrier, inc=1, device_id={"virt": mid}, device_id_type=MESH)
        pl.semaphore_signal(barrier, inc=1, device_id={"copies": other}, device_id_type=MESH)

    pl.semaphore_wait(barrier, 4 + 2 * middle.astype(jnp.int32))

    for c in range(cuts):
        own_inner(c).start()

        @pl.when(middle & full)
        def _():
            own_side(c).start()

    energy_copy.start()
    for c in range(cuts):
        own_next(c).start()
    keep.start()
    for s in range(4):
        column_ref[s] = jnp.transpose(jnp.broadcast_to(row_ref[s], (rows, rows)))[:, 0:1]
    for w in range(2):
        @pl.loop(0, aux // SEND_COLUMNS)
        def _(k):
            cols = pl.ds(pl.multiple_of(k * SEND_COLUMNS, SEND_COLUMNS), SEND_COLUMNS)
            tot[w, :, cols] = jnp.zeros((size, SEND_COLUMNS), jnp.float32)
            ptot[w, :, cols] = jnp.zeros((size, SEND_COLUMNS), jnp.float32)

    keep.wait()

    def inverse(left, i, right, j, r, s):
        return 1.0 / (
            (left[0:1, i : i + 1] + right[0:1, j : j + 1]) - column_ref[r] - row_ref[s]
        )

    def at(i):
        return slice(i * rows, (i + 1) * rows)

    def product(left, source, s, cols, width):
        return jnp.dot(
            left[...], source[s, :, :, cols].reshape(size, width),
            preferred_element_type=jnp.float32,
        )

    def add_columns(total, w, left, source, s):
        @pl.loop(0, aux // SUM_COLUMNS)
        def _(k):
            cols = pl.ds(pl.multiple_of(k * SUM_COLUMNS, SUM_COLUMNS), SUM_COLUMNS)
            total[w, :, cols] += product(left, source, s, cols, SUM_COLUMNS)

    def shard(source, s):
        return source[s].reshape(size, aux)

    def part_arrives(s):
        for c in range(cuts):
            to_next(s, c).wait_recv()

    def pair_ratio(r, s):
        k_ref[...] = contract(shard(own_full, r), shard(own_full, s))
        for i in range(occ):
            for j in range(occ):
                td_ref[at(i), at(j)] = (
                    (2.0 * k_ref[at(i), at(j)] - k_ref[at(j), at(i)])
                    * inverse(e_ref, i, e_ref, j, r, s)
                ).astype(jnp.bfloat16)

    def diagonal(r, s, w):
        pair_ratio(r, s)
        add_columns(tot, w, td_ref, own_full, s)

    def cross(r, s):
        k_ref[...] = contract(shard(part_full, r), shard(own_full, s))
        x_ref[...] = contract(shard(own_full, r), shard(part_full, s))
        for i in range(occ):
            for j in range(occ):
                scale = inverse(e_ref, i, e_part, j, r, s)
                x = x_ref[at(i), at(j)]
                y = k_ref[at(j), at(i)]
                t_ref[at(i), at(j)] = ((2.0 * x - y) * scale).astype(jnp.bfloat16)
                tu_ref[at(j), at(i)] = ((2.0 * y - x) * scale).astype(jnp.bfloat16)

    def spread(s, w):
        add_columns(ptot, w, tu_ref, own_full, s)
        add_columns(tot, w, t_ref, part_full, s)

    def first_half(c):
        @pl.when(gathers)
        def _():
            to_inner(mid, c).wait_recv()

            @pl.when(middle & full)
            def _():
                to_outer(mid, c).start()

            to_next(mid, c).start()

            @pl.when(middle)
            def _():
                to_inner(adj, c).wait_recv()
                to_inner(adj, c).start()

                @pl.when(even)
                def _():
                    to_next(adj, c).start()

            @pl.when(helper)
            def _():
                own_side(c).wait_recv()
                pass_side(c).start()

            @pl.when(end)
            def _():
                to_inner(adj, c).wait_recv()
                to_next(adj, c).start()

    def second_half(c):
        to_inner(tip, c).wait_recv()

        @pl.when(middle)
        def _():
            to_outer(tip, c).start()

        to_next(tip, c).start()

    def send_help(k):
        cols = slice(k * SEND_COLUMNS, (k + 1) * SEND_COLUMNS)
        hsend[k] = ptot[1, :, cols].astype(jnp.bfloat16)
        help_back(k).start()

    def send_result(k):
        cols = slice(k * SEND_COLUMNS, (k + 1) * SEND_COLUMNS)
        help_back(k).wait_recv()
        rsend[k] = (tot[1, :, cols] + hrecv[k].astype(jnp.float32)).astype(jnp.bfloat16)
        result(k).start()

    EARLY = 3
    pair_ratio(v, v)
    first_half(0)
    add_columns(tot, 0, td_ref, own_full, v)
    energy_copy.wait_recv()
    first_half(1)
    first_half(2)
    part_arrives(v)

    @pl.when(end & even)
    def _():
        for c in range(cuts):
            part_to_inner(c).start()

    first_half(3)
    cross(v, v)
    spread(v, 0)

    @pl.loop(4, cuts)
    def _(c):
        first_half(c)

    steps = jnp.where(helper, 5, jnp.where(full, 3, 1))

    @pl.loop(1, steps)
    def _(t):
        assist = helper & ((t == 2) | (t == 3))
        r = jnp.where(assist, adj, v)
        s = jnp.where(t == 1, mid, jnp.where(helper, jnp.where(t == 2, mid, jnp.where(t == 3, v, adj)), adj))
        w = assist.astype(jnp.int32)
        diagonal(r, s, w)
        second_half(2 * t - 2)

        @pl.when(t == 1)
        def _():
            part_arrives(mid)

        @pl.when(t == 2)
        def _():
            part_arrives(adj)

        cross(r, s)
        second_half(2 * t - 1)
        spread(s, w)

        @pl.when(helper & (t == 3))
        def _():
            for k in range(EARLY):
                send_help(k)

    @pl.loop(2 * steps - 2, cuts)
    def _(c):
        second_half(c)

    @pl.when(helper)
    def _():
        for k in range(EARLY, parts):
            send_help(k)
        for k in range(EARLY):
            send_result(k)

    pair_ratio(v, tip)
    part_arrives(tip)
    cross(v, tip)
    for k in chunks:
        cols = slice(k * SEND_COLUMNS, (k + 1) * SEND_COLUMNS)
        psend[k] = (
            ptot[0, :, cols] + product(tu_ref, own_full, tip, cols, SEND_COLUMNS)
        ).astype(jnp.bfloat16)
        back(k).start()

        @pl.when(helper)
        def _():
            if k + EARLY < parts:
                send_result(k + EARLY)

        if by_side(k):
            @pl.when(middle & full)
            def _():
                result(k).wait_recv()
                pass_result(k).start()

    add_columns(tot, 0, td_ref, own_full, tip)
    add_columns(tot, 0, t_ref, part_full, tip)
    for k in chunks:
        cols = slice(k * SEND_COLUMNS, (k + 1) * SEND_COLUMNS)

        @pl.when(served)
        def _():
            pass_result(k).wait_recv()
            tot[0, :, cols] += rrecv[k].astype(jnp.float32)

        back(k).wait_recv()
        staged[k] = (
            (tot[0, :, cols] + precv[k].astype(jnp.float32))
            .astype(jnp.bfloat16)
            .reshape(occ, rows, SEND_COLUMNS)
        )
        write(k).start()

    energy_copy.wait_send()
    for k in chunks:
        back(k).wait_send()
        write(k).wait()

    @pl.loop(0, cuts)
    def _(c):
        to_inner(v, c).wait_send()
        to_next(v, c).wait_send()
        to_next(tip, c).wait_send()

        @pl.when(gathers)
        def _():
            to_next(mid, c).wait_send()

        @pl.when(middle)
        def _():
            to_inner(adj, c).wait_send()
            to_outer(tip, c).wait_send()

        @pl.when((middle & even) | (end & full))
        def _():
            to_next(adj, c).wait_send()

        @pl.when(middle & full)
        def _():
            to_outer(mid, c).wait_send()
            own_side(c).wait_send()

        @pl.when(helper)
        def _():
            pass_side(c).wait_send()

        @pl.when(end & even)
        def _():
            part_to_inner(c).wait_send()

    @pl.when(helper)
    def _():
        for k in chunks:
            help_back(k).wait_send()
            result(k).wait_send()

    @pl.when(middle & full)
    def _():
        for k in chunks:
            if by_side(k):
                pass_result(k).wait_send()


def fused_local(three_index, occ_energy, virt_energy):
    occ, rows, aux = three_index.shape
    members, blocks = lax.axis_size("virt"), lax.axis_size("blk")
    size, parts = occ * rows, aux // SEND_COLUMNS
    vmem = pl.BlockSpec(memory_space=pltpu.VMEM)
    dma = pltpu.SemaphoreType.DMA
    full = pltpu.VMEM((members, occ, rows, aux), jnp.bfloat16)
    total = pltpu.VMEM((2, size, aux), jnp.float32)
    pieces = pltpu.VMEM((parts, size, SEND_COLUMNS), jnp.bfloat16)
    return pl.pallas_call(
        functools.partial(kernel, blocks),
        out_shape=jax.ShapeDtypeStruct((occ, rows, aux), jnp.bfloat16),
        in_specs=[pl.BlockSpec(memory_space=pl.ANY), vmem, vmem],
        out_specs=pl.BlockSpec(memory_space=pl.ANY),
        scratch_shapes=[
            full,
            full,
            pltpu.VMEM((occ, rows, aux), jnp.bfloat16),
            pltpu.VMEM((1, occ), jnp.float32),
            pltpu.VMEM((members, rows, 1), jnp.float32),
            *[total] * 2,
            *[pieces] * 6,
            pltpu.VMEM((parts // 2, size, SEND_COLUMNS), jnp.bfloat16),
            *[pltpu.VMEM((size, size), jnp.float32)] * 2,
            *[pltpu.VMEM((size, size), jnp.bfloat16)] * 3,
            pltpu.VMEM((parts, occ, rows, SEND_COLUMNS), jnp.bfloat16),
            *[dma((members, 2 * occ))] * 3,
            dma((2 * occ,)),
            *[dma((members, 2 * occ))] * 2,
            dma((2, 2 * occ)),
            dma((2 * occ,)),
            *[dma((2, parts))] * 3,
            dma((2, parts // 2)),
            dma((2,)),
            dma((parts,)),
            dma,
        ],
        compiler_params=pltpu.CompilerParams(
            collective_id=0, has_side_effects=True, vmem_limit_bytes=63 * 2**20
        ),
    )(three_index, occ_energy.reshape(1, occ), virt_energy.reshape(members, 1, rows))


def local(three_index, occ_energy, virt_energy):
    occ, rows, aux = three_index.shape
    tiles = rows % 128 == 0 and aux % SUM_COLUMNS == 0 and occ >= 4
    pairs = lax.axis_size("copies") == 2 and lax.axis_size("blk") % 2 == 0
    if tiles and pairs and lax.axis_size("virt") == 4:
        return fused_local(three_index, occ_energy, virt_energy)
    return plain_local(three_index, occ_energy, virt_energy)


def solution(mesh):
    placed = (P(("copies", "blk"), "virt", None), P(("copies", "blk")), P("copies"))
    return jax.shard_map(
        local,
        mesh=mesh,
        in_specs=placed,
        out_specs=P(("copies", "blk"), "virt", None),
        check_vma=False,
    )
```

time: 155 us -> 147 us (0.948)
  the two profiles are of different devices: /device:TPU:0 before, /device:TPU:13 now
where the time goes in v1:
time: 147 us
  Pallas kernels  144 us (98%)
  local copies, waits for them, and re-layouts  3.16 us (2%)
    pallas_call x1, Pallas kernels, fused_local(): pl.pallas_call(functools.partial(kernel, blocks), out_shape=jax.ShapeDtyp...  144 us
    unnamed x1, local copies, waits for them, and re-layouts  3.16 us

profile of v1, /device:TPU:13, one launch (start us, length us, event | category | flops | bytes accessed | tf_op | source)
XLA Modules:
  0.0 147.3 jit_solution(4783629872282015671)
XLA Ops:
  0.0 144.1 %shard_map.37 = bf16[4,128,2048]{2,1,0:T(8,128)(2,1)} custom-call(bf16[4,128,2048]{2,1,0:T(8,128)(2,1)} %a_ref.1, f32[1,4]{1,0:T(1,128)} %bitcast.3, f32[4,1,128]{2,1,0:T(1,128)} %bitcast.2), custom_call_target="tpu_custom_call" | custom-call | tf_op jit(solution)/shard_map/pallas_call | solution.py:530
  144.1 3.2 %copy.5 = bf16[4,128,2048]{2,1,0:T(8,128)(2,1)} copy(bf16[4,128,2048]{2,1,0:T(8,128)(2,1)} %shard_map.37) | data formatting | bytes 4194304

commit v2 on v1

--- a/solution.py
+++ b/solution.py
@@ -10,6 +10,9 @@
 MESH = pl.DeviceIdType.MESH
 SEND_COLUMNS = 256
 SUM_COLUMNS = 1024
+STRIPS = 2
+READY = 3
+PACE = (2, 3, 4, 5, 6, 7, 8)
 
 
 def shifted(shard, axis, by):
@@ -91,10 +94,10 @@
     rel,
     k_ref,
     x_ref,
+    d_ref,
     td_ref,
     tu_ref,
     t_ref,
-    staged,
     send_in,
     send_out,
     send_next,
@@ -108,13 +111,14 @@
     result_sems,
     rel_sems,
     e_sems,
-    out_sems,
     local_sem,
 ):
     occ, rows, aux = a_ref.shape
     size = occ * rows
-    half = aux // 2
-    cuts = 2 * occ
+    high = rows // STRIPS
+    cuts = STRIPS * occ
+    turn = cuts // 8
+    direct = cuts // 2
     parts = aux // SEND_COLUMNS
     chunks = range(parts)
     v = lax.axis_index("virt")
@@ -145,10 +149,11 @@
     def piece(ref, *lead):
         *lead, c = lead
         if isinstance(c, int):
-            i, cols = c // 2, slice((c % 2) * half, (c % 2 + 1) * half)
+            i, first = c // STRIPS, (c % STRIPS) * high
         else:
-            i, cols = c // 2, pl.ds(pl.multiple_of(lax.rem(c, 2) * half, half), half)
-        return ref.at[(*lead, i, slice(None), cols)]
+            i = lax.div(c, STRIPS)
+            first = pl.multiple_of(lax.rem(c, STRIPS) * high, high)
+        return ref.at[(*lead, i, pl.ds(first, high))]
 
     def to_inner(s, c):
         return remote(
@@ -220,10 +225,6 @@
             rel.at[k // 2], rrecv.at[k], rel_sems.at[1, k // 2], result_sems.at[1, k],
             copies=other, virt=adj,
         )
-
-    def write(k):
-        cols = slice(k * SEND_COLUMNS, (k + 1) * SEND_COLUMNS)
-        return pltpu.make_async_copy(staged.at[k], o_ref.at[:, :, cols], out_sems.at[k])
 
     energy_copy = remote(e_ref, e_part, e_sems.at[0], e_sems.at[1], blk=after)
     keep = pltpu.make_async_copy(a_ref, own_full.at[v], local_sem)
@@ -292,10 +293,13 @@
 
     def pair_ratio(r, s):
         k_ref[...] = contract(shard(own_full, r), shard(own_full, s))
+        ratio(k_ref, r, s)
+
+    def ratio(pairs, r, s):
         for i in range(occ):
             for j in range(occ):
                 td_ref[at(i), at(j)] = (
-                    (2.0 * k_ref[at(i), at(j)] - k_ref[at(j), at(i)])
+                    (2.0 * pairs[at(i), at(j)] - pairs[at(j), at(i)])
                     * inverse(e_ref, i, e_ref, j, r, s)
                 ).astype(jnp.bfloat16)
 
@@ -306,13 +310,18 @@
     def cross(r, s):
         k_ref[...] = contract(shard(part_full, r), shard(own_full, s))
         x_ref[...] = contract(shard(own_full, r), shard(part_full, s))
+        amplitudes(r, s)
+
+    def amplitudes(r, s, own=True, partner=True):
         for i in range(occ):
             for j in range(occ):
                 scale = inverse(e_ref, i, e_part, j, r, s)
                 x = x_ref[at(i), at(j)]
                 y = k_ref[at(j), at(i)]
-                t_ref[at(i), at(j)] = ((2.0 * x - y) * scale).astype(jnp.bfloat16)
-                tu_ref[at(j), at(i)] = ((2.0 * y - x) * scale).astype(jnp.bfloat16)
+                if own:
+                    t_ref[at(i), at(j)] = ((2.0 * x - y) * scale).astype(jnp.bfloat16)
+                if partner:
+                    tu_ref[at(j), at(i)] = ((2.0 * y - x) * scale).astype(jnp.bfloat16)
 
     def spread(s, w):
         add_columns(ptot, w, tu_ref, own_full, s)
@@ -334,7 +343,7 @@
                 to_inner(adj, c).wait_recv()
                 to_inner(adj, c).start()
 
-                @pl.when(even)
+                @pl.when(even | (c < direct))
                 def _():
                     to_next(adj, c).start()
 
@@ -358,7 +367,7 @@
         to_next(tip, c).start()
 
     def send_help(k):
-        cols = slice(k * SEND_COLUMNS, (k + 1) * SEND_COLUMNS)
+        cols = pl.ds(pl.multiple_of(k * SEND_COLUMNS, SEND_COLUMNS), SEND_COLUMNS)
         hsend[k] = ptot[1, :, cols].astype(jnp.bfloat16)
         help_back(k).start()
 
@@ -368,70 +377,101 @@
         rsend[k] = (tot[1, :, cols] + hrecv[k].astype(jnp.float32)).astype(jnp.bfloat16)
         result(k).start()
 
-    EARLY = 3
+    def advance(handle, first, last):
+        @pl.loop(first * turn, last * turn)
+        def _(c):
+            handle(c)
+
     pair_ratio(v, v)
-    first_half(0)
+    advance(first_half, 0, 1)
     add_columns(tot, 0, td_ref, own_full, v)
     energy_copy.wait_recv()
-    first_half(1)
-    first_half(2)
+    advance(first_half, 1, 3)
     part_arrives(v)
 
     @pl.when(end & even)
     def _():
-        for c in range(cuts):
+        for c in range(direct, cuts):
             part_to_inner(c).start()
 
-    first_half(3)
+    advance(first_half, 3, 4)
     cross(v, v)
+    advance(first_half, 4, 5)
     spread(v, 0)
-
-    @pl.loop(4, cuts)
-    def _(c):
-        first_half(c)
+    advance(first_half, 5, 8)
+    def paced(t, place):
+        count = 0
+        for index, sent in enumerate(PACE):
+            count = jnp.where(3 * t + place >= 8 + index, sent, count)
+        return jnp.where(helper, count, 0)
+
+    def help_until(t, place):
+        @pl.loop(paced(t, place - 1), paced(t, place))
+        def _(k):
+            send_help(k)
 
     steps = jnp.where(helper, 5, jnp.where(full, 3, 1))
 
     @pl.loop(1, steps)
     def _(t):
-        assist = helper & ((t == 2) | (t == 3))
+        assist = helper & (t < 3)
         r = jnp.where(assist, adj, v)
-        s = jnp.where(t == 1, mid, jnp.where(helper, jnp.where(t == 2, mid, jnp.where(t == 3, v, adj)), adj))
+        s = jnp.where(
+            helper, jnp.where(t == 2, v, jnp.where(t == 4, adj, mid)), jnp.where(t == 1, mid, adj)
+        )
         w = assist.astype(jnp.int32)
-        diagonal(r, s, w)
-        second_half(2 * t - 2)
+        pairs = jnp.where(assist, jnp.where(t == 1, 2, 0), 1)
+
+        @pl.loop(0, pairs)
+        def _(d):
+            diagonal(r, jnp.where(d == 1, v, s), w)
+
+        advance(second_half, 2 * t - 2, 2 * t - 1)
+        help_until(t, 0)
 
         @pl.when(t == 1)
         def _():
             part_arrives(mid)
 
-        @pl.when(t == 2)
+        @pl.when(t == jnp.where(helper, 1, 2))
         def _():
             part_arrives(adj)
 
         cross(r, s)
-        second_half(2 * t - 1)
+        advance(second_half, 2 * t - 1, 2 * t)
+        help_until(t, 1)
         spread(s, w)
-
-        @pl.when(helper & (t == 3))
-        def _():
-            for k in range(EARLY):
-                send_help(k)
-
-    @pl.loop(2 * steps - 2, cuts)
-    def _(c):
-        second_half(c)
+        help_until(t, 2)
+
+    ticks = 2 * steps - 2
+    advance(second_half, ticks, 6)
+
+    def own_pairs(h):
+        block = own_full[tip, pl.ds(h * occ // 2, occ // 2)].reshape(size // 2, aux)
+        columns = slice(h * size // 2, (h + 1) * size // 2)
+        k_ref[:, columns] = contract(shard(part_full, v), block)
+        d_ref[:, columns] = contract(shard(own_full, v), block)
+
+    def part_pairs(h):
+        for c in range(h * cuts // 2, (h + 1) * cuts // 2):
+            to_next(tip, c).wait_recv()
+        block = part_full[tip, pl.ds(h * occ // 2, occ // 2)].reshape(size // 2, aux)
+        x_ref[:, slice(h * size // 2, (h + 1) * size // 2)] = contract(shard(own_full, v), block)
+
+    own_pairs(0)
+    advance(second_half, jnp.maximum(ticks, 6), 7)
+    part_pairs(0)
+    advance(second_half, jnp.maximum(ticks, 7), 8)
 
     @pl.when(helper)
     def _():
-        for k in range(EARLY, parts):
-            send_help(k)
-        for k in range(EARLY):
+        for k in range(READY):
             send_result(k)
 
-    pair_ratio(v, tip)
-    part_arrives(tip)
-    cross(v, tip)
+    own_pairs(1)
+    ratio(d_ref, v, tip)
+    part_pairs(1)
+    amplitudes(v, tip, own=False)
     for k in chunks:
         cols = slice(k * SEND_COLUMNS, (k + 1) * SEND_COLUMNS)
         psend[k] = (
@@ -441,8 +481,8 @@
 
         @pl.when(helper)
         def _():
-            if k + EARLY < parts:
-                send_result(k + EARLY)
+            if k + READY < parts:
+                send_result(k + READY)
 
         if by_side(k):
             @pl.when(middle & full)
@@ -450,6 +490,7 @@
                 result(k).wait_recv()
                 pass_result(k).start()
 
+    amplitudes(v, tip, partner=False)
     add_columns(tot, 0, td_ref, own_full, tip)
     add_columns(tot, 0, t_ref, part_full, tip)
     for k in chunks:
@@ -461,17 +502,15 @@
             tot[0, :, cols] += rrecv[k].astype(jnp.float32)
 
         back(k).wait_recv()
-        staged[k] = (
+        o_ref[:, :, cols] = (
             (tot[0, :, cols] + precv[k].astype(jnp.float32))
             .astype(jnp.bfloat16)
             .reshape(occ, rows, SEND_COLUMNS)
         )
-        write(k).start()
 
     energy_copy.wait_send()
     for k in chunks:
         back(k).wait_send()
-        write(k).wait()
 
     @pl.loop(0, cuts)
     def _(c):
@@ -488,7 +527,7 @@
             to_inner(adj, c).wait_send()
             to_outer(tip, c).wait_send()
 
-        @pl.when((middle & even) | (end & full))
+        @pl.when((middle & (even | (c < direct))) | (end & full))
         def _():
             to_next(adj, c).wait_send()
 
@@ -501,7 +540,7 @@
         def _():
             pass_side(c).wait_send()
 
-        @pl.when(end & even)
+        @pl.when(end & even & (c >= direct))
         def _():
             part_to_inner(c).wait_send()
 
@@ -522,6 +561,7 @@
     occ, rows, aux = three_index.shape
     members, blocks = lax.axis_size("virt"), lax.axis_size("blk")
     size, parts = occ * rows, aux // SEND_COLUMNS
+    cuts = occ * STRIPS
     vmem = pl.BlockSpec(memory_space=pltpu.VMEM)
     dma = pltpu.SemaphoreType.DMA
     full = pltpu.VMEM((members, occ, rows, aux), jnp.bfloat16)
@@ -529,9 +569,9 @@
     pieces = pltpu.VMEM((parts, size, SEND_COLUMNS), jnp.bfloat16)
     return pl.pallas_call(
         functools.partial(kernel, blocks),
-        out_shape=jax.ShapeDtypeStruct((occ, rows, aux), jnp.bfloat16),
+        out_shape=pltpu.VMEM((occ, rows, aux), jnp.bfloat16),
         in_specs=[pl.BlockSpec(memory_space=pl.ANY), vmem, vmem],
-        out_specs=pl.BlockSpec(memory_space=pl.ANY),
+        out_specs=vmem,
         scratch_shapes=[
             full,
             full,
@@ -541,22 +581,20 @@
             *[total] * 2,
             *[pieces] * 6,
             pltpu.VMEM((parts // 2, size, SEND_COLUMNS), jnp.bfloat16),
-            *[pltpu.VMEM((size, size), jnp.float32)] * 2,
+            *[pltpu.VMEM((size, size), jnp.float32)] * 3,
             *[pltpu.VMEM((size, size), jnp.bfloat16)] * 3,
-            pltpu.VMEM((parts, occ, rows, SEND_COLUMNS), jnp.bfloat16),
-            *[dma((members, 2 * occ))] * 3,
-            dma((2 * occ,)),
-            *[dma((members, 2 * occ))] * 2,
-            dma((2, 2 * occ)),
-            dma((2 * occ,)),
+            *[dma((members, cuts))] * 3,
+            dma((cuts,)),
+            *[dma((members, cuts))] * 2,
+            dma((2, cuts)),
+            dma((cuts,)),
             *[dma((2, parts))] * 3,
             dma((2, parts // 2)),
             dma((2,)),
-            dma((parts,)),
             dma,
         ],
         compiler_params=pltpu.CompilerParams(
-            collective_id=0, has_side_effects=True, vmem_limit_bytes=63 * 2**20
+            collective_id=0, has_side_effects=True, vmem_limit_bytes=58 * 2**20
         ),
     )(three_index, occ_energy.reshape(1, occ), virt_energy.reshape(members, 1, rows))
 
@@ -564,8 +602,8 @@
 def local(three_index, occ_energy, virt_energy):
     occ, rows, aux = three_index.shape
     tiles = rows % 128 == 0 and aux % SUM_COLUMNS == 0 and occ >= 4
-    pairs = lax.axis_size("copies") == 2 and lax.axis_size("blk") % 2 == 0
-    if tiles and pairs and lax.axis_size("virt") == 4:
+    paired = lax.axis_size("copies") == 2 and lax.axis_size("blk") % 2 == 0
+    if tiles and paired and occ % 2 == 0 and lax.axis_size("virt") == 4:
         return fused_local(three_index, occ_energy, virt_energy)
     return plain_local(three_index, occ_energy, virt_energy)
 

time: 147 us -> 139 us (0.946)
  the two profiles are of different devices: /device:TPU:13 before, /device:TPU:0 now
where the time goes in v2:
time: 139 us; the launch traced here: 137 us
  Pallas kernels  135 us (97%)
    pallas_call x1, Pallas kernels, fused_local(): pl.pallas_call(functools.partial(kernel, blocks), out_shape=pltpu.VMEM((o...  135 us

profile of v2, /device:TPU:0, one launch (start us, length us, event | category | flops | bytes accessed | tf_op | source)
XLA Modules:
  0.0 136.6 jit_solution(9031307310291295064)
XLA Ops:
  0.0 135.3 %shard_map.37 = bf16[4,128,2048]{2,1,0:T(8,128)(2,1)S(1)} custom-call(bf16[4,128,2048]{2,1,0:T(8,128)(2,1)} %a_ref.1, f32[1,4]{1,0:T(1,128)} %bitcast.3, f32[4,1,128]{2,1,0:T(1,128)} %bitcast.2), custom_call_target="tpu_custom_call" | custom-call | tf_op jit(solution)/shard_map/pallas_call | solution.py:570
  135.3 1.3 copy.5

commit v3 on v2

--- a/solution.py
+++ b/solution.py
@@ -12,7 +12,8 @@
 SUM_COLUMNS = 1024
 STRIPS = 2
 READY = 3
-PACE = (2, 3, 4, 5, 6, 7, 8)
+ASIDE = 3
+PACE = (3, 4, 5, 5, 6, 7, 8)
 
 
 def shifted(shard, axis, by):
@@ -198,14 +199,27 @@
             copies=other, virt=adj,
         )
 
-    def back(k):
-        return remote(
-            psend.at[k], precv.at[k], back_sems.at[0, k], back_sems.at[1, k], blk=before
+    def back(h, k):
+        lines = pl.ds(h * size // 2, size // 2)
+        return remote(
+            psend.at[k, lines], precv.at[k, lines], back_sems.at[0, h, k], back_sems.at[1, h, k],
+            blk=before,
         )
 
     def help_back(k):
         return remote(
             hsend.at[k], hrecv.at[k], help_sems.at[0, k], help_sems.at[1, k], blk=before
+        )
+
+    def help_aside(k):
+        return remote(
+            hsend.at[k], hsend.at[k], help_sems.at[0, k], help_sems.at[1, k], copies=other
+        )
+
+    def pass_help(k):
+        return remote(
+            hsend.at[k], hrecv.at[k], help_sems.at[0, k], help_sems.at[1, k],
+            copies=other, blk=before,
         )
 
     def by_side(k):
@@ -239,8 +253,9 @@
     def _():
         pl.semaphore_signal(barrier, inc=1, device_id={"virt": mid}, device_id_type=MESH)
         pl.semaphore_signal(barrier, inc=1, device_id={"copies": other}, device_id_type=MESH)
-
-    pl.semaphore_wait(barrier, 4 + 2 * middle.astype(jnp.int32))
+        pl.semaphore_signal(barrier, inc=1, device_id={"copies": other, "blk": after}, device_id_type=MESH)
+
+    pl.semaphore_wait(barrier, 4 + 3 * middle.astype(jnp.int32))
 
     for c in range(cuts):
         own_inner(c).start()
@@ -312,9 +327,9 @@
         x_ref[...] = contract(shard(own_full, r), shard(part_full, s))
         amplitudes(r, s)
 
-    def amplitudes(r, s, own=True, partner=True):
+    def amplitudes(r, s, own=True, partner=True, blocks=range(occ)):
         for i in range(occ):
-            for j in range(occ):
+            for j in blocks:
                 scale = inverse(e_ref, i, e_part, j, r, s)
                 x = x_ref[at(i), at(j)]
                 y = k_ref[at(j), at(i)]
@@ -366,10 +381,25 @@
 
         to_next(tip, c).start()
 
-    def send_help(k):
+    def send_help(n):
+        k = lax.rem(n + parts - ASIDE, parts)
         cols = pl.ds(pl.multiple_of(k * SEND_COLUMNS, SEND_COLUMNS), SEND_COLUMNS)
         hsend[k] = ptot[1, :, cols].astype(jnp.bfloat16)
-        help_back(k).start()
+
+        @pl.when(even & (n < ASIDE))
+        def _():
+            help_aside(k).start()
+
+        @pl.when(jnp.logical_not(even & (n < ASIDE)))
+        def _():
+            help_back(k).start()
+
+    def relay_help(first, last):
+        @pl.when(middle & full & even)
+        def _():
+            for k in range(parts - ASIDE + first, parts - ASIDE + last):
+                help_aside(k).wait_recv()
+                pass_help(k).start()
 
     def send_result(k):
         cols = slice(k * SEND_COLUMNS, (k + 1) * SEND_COLUMNS)
@@ -446,11 +476,13 @@
     ticks = 2 * steps - 2
     advance(second_half, ticks, 6)
 
-    def own_pairs(h):
+    def pairs_with_part(h):
         block = own_full[tip, pl.ds(h * occ // 2, occ // 2)].reshape(size // 2, aux)
-        columns = slice(h * size // 2, (h + 1) * size // 2)
-        k_ref[:, columns] = contract(shard(part_full, v), block)
-        d_ref[:, columns] = contract(shard(own_full, v), block)
+        k_ref[:, slice(h * size // 2, (h + 1) * size // 2)] = contract(shard(part_full, v), block)
+
+    def pairs_with_own(h):
+        block = own_full[tip, pl.ds(h * occ // 2, occ // 2)].reshape(size // 2, aux)
+        d_ref[:, slice(h * size // 2, (h + 1) * size // 2)] = contract(shard(own_full, v), block)
 
     def part_pairs(h):
         for c in range(h * cuts // 2, (h + 1) * cuts // 2):
@@ -458,8 +490,11 @@
         block = part_full[tip, pl.ds(h * occ // 2, occ // 2)].reshape(size // 2, aux)
         x_ref[:, slice(h * size // 2, (h + 1) * size // 2)] = contract(shard(own_full, v), block)
 
-    own_pairs(0)
+    relay_help(0, ASIDE // 2)
+    pairs_with_part(0)
+    pairs_with_own(0)
     advance(second_half, jnp.maximum(ticks, 6), 7)
+    relay_help(ASIDE // 2, ASIDE)
     part_pairs(0)
     advance(second_half, jnp.maximum(ticks, 7), 8)
 
@@ -468,21 +503,29 @@
         for k in range(READY):
             send_result(k)
 
-    own_pairs(1)
+    def send_back(h, k):
+        cols = slice(k * SEND_COLUMNS, (k + 1) * SEND_COLUMNS)
+        lines = slice(h * size // 2, (h + 1) * size // 2)
+        psend[k, lines] = (
+            ptot[0, lines, cols] + product(tu_ref.at[lines], own_full, tip, cols, SEND_COLUMNS)
+        ).astype(jnp.bfloat16)
+        back(h, k).start()
+
+    @pl.when(helper)
+    def _():
+        for k in range(READY, parts):
+            send_result(k)
+
+    pairs_with_part(1)
+    amplitudes(v, tip, own=False, blocks=range(occ // 2))
+    for k in chunks:
+        send_back(0, k)
+    pairs_with_own(1)
     ratio(d_ref, v, tip)
     part_pairs(1)
-    amplitudes(v, tip, own=False)
+    amplitudes(v, tip, own=False, blocks=range(occ // 2, occ))
     for k in chunks:
-        cols = slice(k * SEND_COLUMNS, (k + 1) * SEND_COLUMNS)
-        psend[k] = (
-            ptot[0, :, cols] + product(tu_ref, own_full, tip, cols, SEND_COLUMNS)
-        ).astype(jnp.bfloat16)
-        back(k).start()
-
-        @pl.when(helper)
-        def _():
-            if k + READY < parts:
-                send_result(k + READY)
+        send_back(1, k)
 
         if by_side(k):
             @pl.when(middle & full)
@@ -493,6 +536,7 @@
     amplitudes(v, tip, partner=False)
     add_columns(tot, 0, td_ref, own_full, tip)
     add_columns(tot, 0, t_ref, part_full, tip)
+
     for k in chunks:
         cols = slice(k * SEND_COLUMNS, (k + 1) * SEND_COLUMNS)
 
@@ -501,7 +545,8 @@
             pass_result(k).wait_recv()
             tot[0, :, cols] += rrecv[k].astype(jnp.float32)
 
-        back(k).wait_recv()
+        for h in range(2):
+            back(h, k).wait_recv()
         o_ref[:, :, cols] = (
             (tot[0, :, cols] + precv[k].astype(jnp.float32))
             .astype(jnp.bfloat16)
@@ -510,7 +555,8 @@
 
     energy_copy.wait_send()
     for k in chunks:
-        back(k).wait_send()
+        for h in range(2):
+            back(h, k).wait_send()
 
     @pl.loop(0, cuts)
     def _(c):
@@ -555,6 +601,11 @@
         for k in chunks:
             if by_side(k):
                 pass_result(k).wait_send()
+
+    @pl.when(middle & full & even)
+    def _():
+        for k in range(parts - ASIDE, parts):
+            pass_help(k).wait_send()
 
 
 def fused_local(three_index, occ_energy, virt_energy):
@@ -588,7 +639,8 @@
             *[dma((members, cuts))] * 2,
             dma((2, cuts)),
             dma((cuts,)),
-            *[dma((2, parts))] * 3,
+            dma((2, 2, parts)),
+            *[dma((2, parts))] * 2,
             dma((2, parts // 2)),
             dma((2,)),
             dma,

time: 139 us -> 136 us (0.978)
  Pallas kernels: 135 us -> 133 us
    pallas_call x1, Pallas kernels: 135 us -> 133 us  [fused_local(): pl.pallas_call(functools.partial(kernel, blocks), out_shape=pltpu.VMEM((o...]
where the time goes in v3:
time: 136 us; the launch traced here: 134 us
  Pallas kernels  133 us (98%)
    pallas_call x1, Pallas kernels, fused_local(): pl.pallas_call(functools.partial(kernel, blocks), out_shape=pltpu.VMEM((o...  133 us

profile of v3, /device:TPU:0, one launch (start us, length us, event | category | flops | bytes accessed | tf_op | source)
XLA Modules:
  0.0 133.9 jit_solution(10743346235820607064)
XLA Ops:
  0.0 132.5 %shard_map.37 = bf16[4,128,2048]{2,1,0:T(8,128)(2,1)S(1)} custom-call(bf16[4,128,2048]{2,1,0:T(8,128)(2,1)} %a_ref.1, f32[1,4]{1,0:T(1,128)} %bitcast.3, f32[4,1,128]{2,1,0:T(1,128)} %bitcast.2), custom_call_target="tpu_custom_call" | custom-call | tf_op jit(solution)/shard_map/pallas_call | solution.py:621
  132.5 1.3 copy.5

commit v4 on v3

--- a/solution.py
+++ b/solution.py
@@ -223,7 +223,7 @@
         )
 
     def by_side(k):
-        return k % 2 == 1
+        return k % 2 == 1 and k < parts - 1
 
     def result(k):
         if by_side(k):

time: 136 us -> 135 us (level)
  no operation moved by 1% of the time
where the time goes in v4:
time: 135 us; the launch traced here: 134 us
  Pallas kernels  133 us (99%)
    pallas_call x1, Pallas kernels, fused_local(): pl.pallas_call(functools.partial(kernel, blocks), out_shape=pltpu.VMEM((o...  133 us

profile of v4, /device:TPU:0, one launch (start us, length us, event | category | flops | bytes accessed | tf_op | source)
XLA Modules:
  0.0 133.9 jit_solution(7880913226555775688)
XLA Ops:
  0.0 132.5 %shard_map.37 = bf16[4,128,2048]{2,1,0:T(8,128)(2,1)S(1)} custom-call(bf16[4,128,2048]{2,1,0:T(8,128)(2,1)} %a_ref.1, f32[1,4]{1,0:T(1,128)} %bitcast.3, f32[4,1,128]{2,1,0:T(1,128)} %bitcast.2), custom_call_target="tpu_custom_call" | custom-call | tf_op jit(solution)/shard_map/pallas_call | solution.py:621
  132.5 1.3 copy.5

commit v5 on v4

--- a/solution.py
+++ b/solution.py
@@ -247,7 +247,6 @@
     pl.semaphore_signal(barrier, inc=1, device_id={"blk": after}, device_id_type=MESH)
     pl.semaphore_signal(barrier, inc=1, device_id={"blk": before}, device_id_type=MESH)
     pl.semaphore_signal(barrier, inc=1, device_id={"virt": adj}, device_id_type=MESH)
-    pl.semaphore_signal(barrier, inc=1, device_id={"copies": other, "virt": adj}, device_id_type=MESH)
 
     @pl.when(middle)
     def _():
@@ -255,7 +254,7 @@
         pl.semaphore_signal(barrier, inc=1, device_id={"copies": other}, device_id_type=MESH)
         pl.semaphore_signal(barrier, inc=1, device_id={"copies": other, "blk": after}, device_id_type=MESH)
 
-    pl.semaphore_wait(barrier, 4 + 3 * middle.astype(jnp.int32))
+    pl.semaphore_wait(barrier, 3 + 3 * middle.astype(jnp.int32))
 
     for c in range(cuts):
         own_inner(c).start()

time: 135 us -> 135 us (level)
  no operation moved by 1% of the time
where the time goes in v5:
time: 135 us; the launch traced here: 134 us
  Pallas kernels  133 us (99%)
    pallas_call x1, Pallas kernels, fused_local(): pl.pallas_call(functools.partial(kernel, blocks), out_shape=pltpu.VMEM((o...  133 us

profile of v5, /device:TPU:0, one launch (start us, length us, event | category | flops | bytes accessed | tf_op | source)
XLA Modules:
  0.0 133.9 jit_solution(5980065119715423062)
XLA Ops:
  0.0 132.5 %shard_map.37 = bf16[4,128,2048]{2,1,0:T(8,128)(2,1)S(1)} custom-call(bf16[4,128,2048]{2,1,0:T(8,128)(2,1)} %a_ref.1, f32[1,4]{1,0:T(1,128)} %bitcast.3, f32[4,1,128]{2,1,0:T(1,128)} %bitcast.2), custom_call_target="tpu_custom_call" | custom-call | tf_op jit(solution)/shard_map/pallas_call | solution.py:620
  132.6 1.3 copy.5
